TPU v7x, 32 devices: a whole 2x2x4 slice. The times are simulated.
32 devices in a mesh: pages: 2 (over y), rows: 4 (over x, core), cols: 4 (over z).
Axes of the slice: x: 2, y: 2, z: 4, core: 2. Of those that a mesh axis runs over, the one named last changes fastest.
Arguments:
- features: bfloat16 [128, 64, 768], P(('pages', 'rows'), 'cols'), parts along dimension 0, may hold values from -6 to 6
- dw_kernel: bfloat16 [31, 31, 768], P(None, None, ('rows', 'cols')), may hold values from -0.1875 to 0.1875
- w_up: bfloat16 [768, 1536], P(None, ('rows', 'cols')), may hold values from -0.21875 to 0.21875
- w_down: bfloat16 [768, 1536], P(None, ('rows', 'cols')), may hold values from -0.15625 to 0.15625
Outputs:
- block_out: bfloat16 [128, 64, 768], P(('pages', 'rows'), 'cols'), parts along dimension 0
There are 2 independent parts, one for each index of `pages`. A program takes and returns all parts, laid end to end along the dimension named above; an argument that names none is the same for every part. Nothing has to cross between parts.
All inputs are finite; a program needn't handle non-finite values.
Results may differ from a plain program's by a relative error of at most 0.0053.
Values may be sent and summed in bfloat16 or wider, within the bound.
No kernel may reach another device: no remote copies, remote signals or barrier semaphores. Data moves between devices by JAX's collectives and lax.ppermute only.
A program may use at most 64 MiB of HBM per device.

v0:
```python
import jax
import jax.numpy as jnp
from jax import lax
from jax.sharding import PartitionSpec as P


def extended(block, sides, width):
    for axis, dim in sides:
        count = lax.axis_size(axis)
        forward = [(i, i + 1) for i in range(count - 1)]
        backward = [(target, source) for source, target in forward]
        low = lax.ppermute(
            lax.slice_in_dim(block, block.shape[dim] - width, None, axis=dim), axis, forward
        )
        high = lax.ppermute(lax.slice_in_dim(block, 0, width, axis=dim), axis, backward)
        block = jnp.concatenate([low, block, high], axis=dim)
    return block


def expand(normed_rows, piece):
    return jax.nn.gelu(
        jnp.dot(normed_rows, piece, preferred_element_type=jnp.float32), approximate=False
    ).astype(jnp.bfloat16)


def reduce_back(hidden, piece):
    return lax.dot_general(
        hidden, piece, (((1,), (1,)), ((), ())), preferred_element_type=jnp.float32
    )


def on_device(features, dw_kernel, w_up, w_down):
    tile_rows, tile_cols, channels = features.shape
    taps = lax.all_gather(dw_kernel, ("rows", "cols"), axis=2, tiled=True)
    side = taps.shape[0]
    half = (side - 1) // 2
    padded = extended(features, (("rows", 0), ("cols", 1)), half)
    kernel = taps.reshape(side, side, 1, channels)
    mixed = lax.conv_general_dilated(
        padded[None],
        kernel,
        (1, 1),
        "VALID",
        dimension_numbers=("NHWC", "HWIO", "NHWC"),
        feature_group_count=channels,
        preferred_element_type=jnp.float32,
    )[0]
    spread = (features.astype(jnp.float32) + mixed).astype(jnp.bfloat16)
    values = spread.reshape(tile_rows * tile_cols, channels).astype(jnp.float32)
    center = jnp.mean(values, axis=1, keepdims=True)
    spread_sq = jnp.mean((values - center) ** 2, axis=1, keepdims=True)
    normed = ((values - center) * lax.rsqrt(spread_sq + 1e-06)).astype(jnp.bfloat16)
    hidden = expand(normed, lax.all_gather(w_up, ("rows", "cols"), axis=1, tiled=True))
    ffn = reduce_back(hidden, lax.all_gather(w_down, ("rows", "cols"), axis=1, tiled=True))
    result = (values + ffn).astype(jnp.bfloat16)
    return result.reshape(tile_rows, tile_cols, channels)


def solution(mesh):
    return jax.shard_map(
        on_device,
        mesh=mesh,
        in_specs=(
            P(("pages", "rows"), "cols", None),
            P(None, None, ("rows", "cols")),
            P(None, ("rows", "cols")),
            P(None, ("rows", "cols")),
        ),
        out_specs=P(("pages", "rows"), "cols", None),
        check_vma=False,
    )
```

profile of v0, /device:TPU:0, one launch (start us, length us, event | category | flops | bytes accessed | tf_op | source)
XLA Modules:
  0.0 190.2 jit_solution(11549319365002684334)
XLA Ops:
  6.5 0.0 copy-start
  6.5 0.0 all-gather.4.cloned.1.call-start
  6.5 2.4 %copy.11 = bf16[31,31,48]{1,0,2:T(8,128)(2,1)} copy(bf16[31,31,48]{2,1,0:T(8,128)(2,1)} %param.5) | data formatting | bytes 184512 | tf_op args[1]
  9.0 0.0 all-gather.4.cloned.1.call-update
  9.0 0.0 all-gather.8.cloned.1.call-start
  9.0 0.7 all-gather.8.cloned.1.call-update
  9.7 0.0 all-gather.6.cloned.1.call-start
  9.8 0.0 copy-done
  9.8 0.1 fusion.78
  9.9 2.4 %collective-permute-start = (bf16[15,16,768]{2,1,0:T(8,128)(2,1)S(1)}, bf16[15,16,768]{2,1,0:T(8,128)(2,1)S(1)}, u32[]{:S(2)}, u32[]{:S(2)}) collective-permute-start(bf16[15,16,768]{2,1,0:T(8,128)(2,1)S(1)} %get-tuple-element.10), channel_id=1, source_target_pairs={{0,4},{4,8},{8,12},{1,5},{5,9},{9,13},{2,6},{6,10},{10,14},{3,7},{... | collective-permute-start | bytes 1105928 | tf_op jit(solution)/shard_map/ppermute | solution.py:12
  12.3 1.3 collective-permute-start.1
  13.6 0.0 collective-permute-done
  13.7 4.3 %collective-permute-done.1 = bf16[15,16,768]{2,1,0:T(8,128)(2,1)S(1)} collective-permute-done((bf16[15,16,768]{2,1,0:T(8,128)(2,1)S(1)}, bf16[15,16,768]{2,1,0:T(8,128)(2,1)S(1)}, u32[]{:S(2)}, u32[]{:S(2)}) %collective-permute-start.1) | collective-permute-done | bytes 368672 | tf_op jit(solution)/shard_map/ppermute | solution.py:15
  18.0 0.5 fusion.77
  18.4 0.3 copy.8
  18.8 1.3 collective-permute-start.3
  20.1 1.4 copy.7
  21.5 5.5 %collective-permute-start.2 = (bf16[46,15,768]{2,0,1:T(8,128)(2,1)}, bf16[46,15,768]{2,0,1:T(8,128)(2,1)}, u32[]{:S(2)}, u32[]{:S(2)}) collective-permute-start(bf16[46,15,768]{2,0,1:T(8,128)(2,1)} %copy.7), channel_id=1, source_target_pairs={{0,1},{1,2},{2,3},{4,5},{5,6},{6,7},{8,9},{9,10},{10,11},{12,13},{... | collective-permute-start | bytes 3179528 | tf_op jit(solution)/shard_map/ppermute | solution.py:12
  27.0 0.0 all-gather.6.cloned.1.call-update
  27.0 39.9 %collective-permute-done.3 = bf16[46,15,768]{2,0,1:T(8,128)(2,1)} collective-permute-done((bf16[46,15,768]{2,0,1:T(8,128)(2,1)S(1)}, bf16[46,15,768]{2,0,1:T(8,128)(2,1)}, u32[]{:S(2)}, u32[]{:S(2)}) %collective-permute-start.3) | collective-permute-done | bytes 1059872 | tf_op jit(solution)/shard_map/ppermute | solution.py:15
  67.0 1.6 copy.10
  68.5 0.0 collective-permute-done.2
  68.6 1.6 copy.9
  70.1 2.6 %maximum_bitcast_fusion = bf16[1,46,46,768]{3,2,1,0:T(8,128)(2,1)} fusion(bf16[46,15,768]{2,1,0:T(8,128)(2,1)S(1)} %copy.10, bf16[46,16,768]{2,1,0:T(8,128)(2,1)S(1)} %constant_dynamic-update-slice_fusion, bf16[46,15,768]{2,1,0:T(8,128)(2,1)S(1)} %copy.9), kind=kLoop, calls=%fused_computation.2 | loop fusion | flops 9750528 | bytes 6500352 | tf_op jit(solution)/shard_map/broadcast_in_dim | solution.py:40
  72.8 14.1 %all-gather.4.cloned.1.call-done = bf16[31,31,768]{1,0,2:T(8,128)(2,1)} async-done(((bf16[31,31,48]{1,0,2:T(8,128)(2,1)}), bf16[31,31,768]{1,0,2:T(8,128)(2,1)}) %all-gather.4.cloned.1.call-update) | async-done | bytes 1476112 | tf_op jit(solution)/shard_map/all_gather | solution.py:34
  86.8 0.0 copy-start.2
  86.8 12.8 %copy.14 = bf16[31,31,1,768]{3,2,1,0:T(2,128)(2,1)} copy(bf16[31,31,1,768]{1,0,3,2:T(8,128)(2,1)} %bitcast.20) | data formatting | bytes 2952192 | tf_op jit(solution)/shard_map/reshape | solution.py:38
  99.6 0.0 copy-done.2
  99.6 0.0 copy-start.1
  99.6 75.5 %fusion = f32[1,16,16,768]{3,0,2,1:T(1,128)S(1)} fusion(bf16[31,31,1,768]{3,2,1,0:T(2,128)(2,1)} %copy.14, bf16[1,46,46,768]{3,2,1,0:T(8,128)(2,1)S(1)} %copy-done.2), kind=kOutput, calls=%fused_computation | convolution fusion | flops 377880576 | bytes 5512704 | tf_op jit(solution)/shard_map/conv_general_dilated | solution.py:39
  175.1 0.0 copy-done.1
  175.1 0.2 convert_reduce_fusion
  175.3 0.1 div.9
  175.4 0.2 multiply_reduce_fusion
  175.6 0.1 rsqrt.12
  175.7 0.2 fusion.15
  175.9 0.0 all-gather.8.cloned.1.call-done
  176.0 0.0 all-gather.6.cloned.1.call-done
  176.0 7.7 %fusion.12 = bf16[256,768]{1,0:T(8,128)(2,1)} fusion(bf16[768,1536]{0,1:T(8,128)(2,1)} %all-gather.8.cloned.1.call-done, bf16[256,768]{1,0:T(8,128)(2,1)S(1)} %fusion.15, bf16[768,1536]{0,1:T(8,128)(2,1)} %all-gather.6.cloned.1.call-done, bf16[256,768]{1,0:T(8,128)(2,1)S(1)} %bitcast.21), kind=kOutput, calls=%fused_computation.23 | convolution fusion | flops 1234108416 | bytes 5898240 | tf_op jit(solution)/shard_map/dot_general | solution.py:27
  (5 shorter events, 0.1 us)
Async XLA Ops:
  6.5 3.3 %copy-start = (bf16[16,16,768]{2,1,0:T(8,128)(2,1)S(1)}, bf16[16,16,768]{2,1,0:T(8,128)(2,1)}, u32[]{:S(2)}) copy-start(bf16[16,16,768]{2,1,0:T(8,128)(2,1)} %param.4) | copy-start | bytes 1179652
  6.5 80.3 %all-gather.4.cloned.1.call-start = ((), (), s32[]{:S(2)}) async-start(), calls=%async_computation | async-start | bytes 6684672 | tf_op jit(solution)/shard_map/all_gather | solution.py:34
  9.0 167.0 %all-gather.8.cloned.1.call-start = ((), (), s32[]{:S(2)}) async-start(), calls=%async_computation.2 | async-start | bytes 2506752 | tf_op jit(solution)/shard_map/all_gather | solution.py:54
  9.7 166.2 %all-gather.6.cloned.1.call-start = ((), (), s32[]{:S(2)}) async-start(), calls=%async_computation.1 | async-start | bytes 2506752 | tf_op jit(solution)/shard_map/all_gather | solution.py:53
  9.9 3.7 %collective-permute-start = (bf16[15,16,768]{2,1,0:T(8,128)(2,1)S(1)}, bf16[15,16,768]{2,1,0:T(8,128)(2,1)S(1)}, u32[]{:S(2)}, u32[]{:S(2)}) collective-permute-start(bf16[15,16,768]{2,1,0:T(8,128)(2,1)S(1)} %get-tuple-element.10), channel_id=1, source_target_pairs={{0,4},{4,8},{8,12},{1,5},{5,9},{9,13},{2,6},{6,10},{10,14},{3,7},{... | collective-permute-start | bytes 1105928 | tf_op jit(solution)/shard_map/ppermute | solution.py:12
  12.3 5.7 %collective-permute-start.1 = (bf16[15,16,768]{2,1,0:T(8,128)(2,1)S(1)}, bf16[15,16,768]{2,1,0:T(8,128)(2,1)S(1)}, u32[]{:S(2)}, u32[]{:S(2)}) collective-permute-start(bf16[15,16,768]{2,1,0:T(8,128)(2,1)S(1)} %get-tuple-element.9), channel_id=1, source_target_pairs={{4,0},{8,4},{12,8},{5,1},{9,5},{13,9},{6,2},{10,6},{14,10},{7,3},{... | collective-permute-start | bytes 1105928 | tf_op jit(solution)/shard_map/ppermute | solution.py:15
  18.8 48.2 %collective-permute-start.3 = (bf16[46,15,768]{2,0,1:T(8,128)(2,1)S(1)}, bf16[46,15,768]{2,0,1:T(8,128)(2,1)}, u32[]{:S(2)}, u32[]{:S(2)}) collective-permute-start(bf16[46,15,768]{2,0,1:T(8,128)(2,1)S(1)} %copy.8), channel_id=1, source_target_pairs={{1,0},{2,1},{3,2},{5,4},{6,5},{7,6},{9,8},{10,9},{11,10},{13,12},{... | collective-permute-start | bytes 3179528 | tf_op jit(solution)/shard_map/ppermute | solution.py:15
  21.5 47.1 %collective-permute-start.2 = (bf16[46,15,768]{2,0,1:T(8,128)(2,1)}, bf16[46,15,768]{2,0,1:T(8,128)(2,1)}, u32[]{:S(2)}, u32[]{:S(2)}) collective-permute-start(bf16[46,15,768]{2,0,1:T(8,128)(2,1)} %copy.7), channel_id=1, source_target_pairs={{0,1},{1,2},{2,3},{4,5},{5,6},{6,7},{8,9},{9,10},{10,11},{12,13},{... | collective-permute-start | bytes 3179528 | tf_op jit(solution)/shard_map/ppermute | solution.py:12
  86.8 12.8 %copy-start.2 = (bf16[1,46,46,768]{3,2,1,0:T(8,128)(2,1)S(1)}, bf16[1,46,46,768]{3,2,1,0:T(8,128)(2,1)}, u32[]{:S(2)}) copy-start(bf16[1,46,46,768]{3,2,1,0:T(8,128)(2,1)} %maximum_bitcast_fusion) | copy-start | bytes 9750532
  99.6 75.5 %copy-start.1 = (bf16[16,16,768]{2,1,0:T(8,128)(2,1)S(1)}, bf16[16,16,768]{2,1,0:T(8,128)(2,1)}, u32[]{:S(2)}) copy-start(bf16[16,16,768]{2,1,0:T(8,128)(2,1)} %param.4) | copy-start | bytes 1179652
Sparse Core Ops, SparseCore 0:
  9.6 77.1 all-gather.3
  89.1 42.1 all-gather.7
  133.7 41.0 all-gather.5
where the time goes:
time: 191 us; the launch traced here: 190 us
  matrix products  83.2 us (44%)
  waiting for transfers between devices  59 us (31%)
  local copies, waits for them, and re-layouts  20.9 us (11%)
  between operations  13.2 us (7%)
  starting transfers between devices  10.6 us (6%)
  other arithmetic  3.25 us (2%)
    conv_general_dilated x1, matrix products, on_device(): lax.conv_general_dilated(padded[None], kernel, (1, 1), 'VALID', dimension...  75.5 us
    ppermute x2, waiting for transfers between devices, extended(): lax.ppermute(lax.slice_in_dim(block, 0, width, axis=dim), axis, backward)  44.2 us
    all_gather x1, waiting for transfers between devices, on_device(): taps = lax.all_gather(dw_kernel, ('rows', 'cols'), axis=2, tiled=True)  14.1 us
    reshape x1, local copies, waits for them, and re-layouts, on_device(): kernel = taps.reshape(side, side, 1, channels)  12.8 us
    ppermute x2, starting transfers between devices, extended(): lax.ppermute(lax.slice_in_dim(block, block.shape[dim] - width, None, axis...  7.96 us
    dot_general x1, matrix products, reduce_back(): lax.dot_general(hidden, piece, (((1,), (1,)), ((), ())), preferred_elemen...  7.72 us
  transfers between devices with their start and end apart: 7, of which 3 were waited for; matrix products, arithmetic and copies ran while one was open for 51% of the time, Pallas kernels for 0%

commit v1 on v0

--- a/solution.py
+++ b/solution.py
@@ -31,7 +31,29 @@
 
 def on_device(features, dw_kernel, w_up, w_down):
     tile_rows, tile_cols, channels = features.shape
-    taps = lax.all_gather(dw_kernel, ("rows", "cols"), axis=2, tiled=True)
+    ways, here, turn = (
+        lax.axis_size(("rows", "cols")),
+        lax.axis_index(("rows", "cols")),
+        dw_kernel.shape[2],
+    )
+    shape = [n * ways if d == 2 else n for d, n in enumerate(dw_kernel.shape)]
+    full = lax.dynamic_update_slice_in_dim(
+        jnp.zeros(shape, dw_kernel.dtype), dw_kernel, here * turn, axis=2
+    )
+    going_up = going_down = dw_kernel
+    for far in range(1, ways // 2 + 1):
+        going_up = lax.ppermute(
+            going_up, ("rows", "cols"), [(d, (d + 1) % ways) for d in range(ways)]
+        )
+        full = lax.dynamic_update_slice_in_dim(full, going_up, (here - far) % ways * turn, axis=2)
+        if 2 * far < ways:
+            going_down = lax.ppermute(
+                going_down, ("rows", "cols"), [(d, (d - 1) % ways) for d in range(ways)]
+            )
+            full = lax.dynamic_update_slice_in_dim(
+                full, going_down, (here + far) % ways * turn, axis=2
+            )
+    taps = full
     side = taps.shape[0]
     half = (side - 1) // 2
     padded = extended(features, (("rows", 0), ("cols", 1)), half)

time: 191 us -> 2620 us (13.72)
  local copies, waits for them, and re-layouts: 20.9 us -> 2370 us
  waiting for transfers between devices: 59 us -> 106 us
    dynamic_update_slice x0 -> x16, local copies, waits for them, and re-layouts: none -> 2340 us  [the longest x8 1170 us: on_device(): lax.dynamic_update_slice_in_dim(full, going_up, (here - far) % ways * tur...]
    ppermute x0 -> x15, waiting for transfers between devices: none -> 101 us  [the longest x8 63.3 us: on_device(): lax.ppermute(going_up, ('rows', 'cols'), [(d, (d + 1) % ways) for d in ra...]
    ppermute x2, waiting for transfers between devices: 44.2 us -> 4.27 us  [extended(): lax.ppermute(lax.slice_in_dim(block, 0, width, axis=dim), axis, backward)]
  transfers between devices with their start and end apart: 7 -> 21, of which waited for: 3 -> 14; matrix products, arithmetic and copies ran while one was open for 51% -> 94% of each run, Pallas kernels for 0% -> 0%
where the time goes in v1:
time: 2620 us; the launch traced here: 2600 us
  local copies, waits for them, and re-layouts  2370 us (90%)
  waiting for transfers between devices  106 us (4%)
  matrix products  83.3 us (3%)
    dynamic_update_slice x8, local copies, waits for them, and re-layouts, on_device(): lax.dynamic_update_slice_in_dim(full, going_up, (here - far) % ways * tur...  1170 us
    dynamic_update_slice x7, local copies, waits for them, and re-layouts, on_device(): lax.dynamic_update_slice_in_dim(full, going_down, (here + far) % ways * t...  1140 us
    conv_general_dilated x1, matrix products, on_device(): lax.conv_general_dilated(padded[None], kernel, (1, 1), 'VALID', dimension...  75.6 us
    ppermute x8, waiting for transfers between devices, on_device(): lax.ppermute(going_up, ('rows', 'cols'), [(d, (d + 1) % ways) for d in ra...  63.3 us
  transfers between devices with their start and end apart: 21, of which 14 were waited for; matrix products, arithmetic and copies ran while one was open for 94% of the time, Pallas kernels for 0%

profile of v1, /device:TPU:0, one launch (start us, length us, event | category | flops | bytes accessed | tf_op | source)
XLA Modules:
  0.0 2599.8 jit_solution(3536918129881979261)
XLA Ops:
  8.5 2.4 collective-permute-start
  12.3 4.3 collective-permute-done.1
  17.4 4.6 collective-permute-start.2
  22.1 1.4 copy.39
  24.8 2.7 collective-permute-start.4
  27.5 1.8 collective-permute-start.5
  29.3 37.7 %collective-permute-done.4 = bf16[31,31,48]{2,1,0:T(8,128)(2,1)} collective-permute-done((bf16[31,31,48]{2,1,0:T(8,128)(2,1)S(1)}, bf16[31,31,48]{2,1,0:T(8,128)(2,1)}, u32[]{:S(2)}, u32[]{:S(2)}) %collective-permute-start.4) | collective-permute-done | bytes 92288 | tf_op jit(solution)/shard_map/ppermute | solution.py:45
  66.9 2.3 collective-permute-done.5
  69.3 2.2 collective-permute-start.7
  71.5 6.8 collective-permute-done.6
  78.4 2.5 collective-permute-done.7
  80.8 2.1 collective-permute-start.9
  83.0 6.4 collective-permute-done.8
  89.4 5.0 collective-permute-done.9
  95.1 5.2 collective-permute-done.10
  100.3 7.2 collective-permute-done.11
  107.5 4.0 collective-permute-done.12
  111.5 9.8 collective-permute-done.13
  121.3 1.9 collective-permute-done.14
  123.3 10.5 collective-permute-done.15
  136.7 3.1 reshape.105
  139.8 34.9 %dynamic_update_slice.64 = bf16[31,31,1,768]{3,2,1,0:T(2,128)(2,1)} dynamic-update-slice(bf16[31,31,1,768]{3,2,1,0:T(2,128)(2,1)} %reshape.105, bf16[31,31,1,48]{3,2,1,0:T(2,128)(2,1)S(1)} %copy.42, s32[]{:T(128)} %constant.145.clone.1, s32[]{:T(128)} %constant.145.clone.1, s32[]{:T(128)} %constant.145.clone.1, s32[]{:T(128)S(6)} %select_n.111) | dynamic-update-slice | bytes 184516 | tf_op jit(solution)/shard_map/dynamic_update_slice | solution.py:40
  176.1 1.3 copy.44
  177.5 162.0 %dynamic_update_slice.65 = bf16[31,31,1,768]{3,2,1,0:T(2,128)(2,1)} dynamic-update-slice(bf16[31,31,1,768]{3,2,1,0:T(2,128)(2,1)} %dynamic_update_slice.64, bf16[31,31,1,48]{3,2,1,0:T(2,128)(2,1)S(1)} %copy.43, s32[]{:T(128)} %constant.145.clone.1, s32[]{:T(128)} %constant.145.clone.1, s32[]{:T(128)} %constant.145.clone.1, s32[]{:T(128)S(6)} %select_n.113) | dynamic-update-slice | bytes 184516 | tf_op jit(solution)/shard_map/dynamic_update_slice | solution.py:48
  339.4 162.5 %dynamic_update_slice.66 = bf16[31,31,1,768]{3,2,1,0:T(2,128)(2,1)} dynamic-update-slice(bf16[31,31,1,768]{3,2,1,0:T(2,128)(2,1)} %dynamic_update_slice.65, bf16[31,31,1,48]{3,2,1,0:T(2,128)(2,1)S(1)} %copy.44, s32[]{:T(128)} %constant.145.clone.1, s32[]{:T(128)} %constant.145.clone.1, s32[]{:T(128)} %constant.145.clone.1, s32[]{:T(128)S(6)} %select_n.115) | dynamic-update-slice | bytes 184516 | tf_op jit(solution)/shard_map/dynamic_update_slice | solution.py:53
  503.3 1.3 copy.46
  504.6 162.0 %dynamic_update_slice.67 = bf16[31,31,1,768]{3,2,1,0:T(2,128)(2,1)} dynamic-update-slice(bf16[31,31,1,768]{3,2,1,0:T(2,128)(2,1)} %dynamic_update_slice.66, bf16[31,31,1,48]{3,2,1,0:T(2,128)(2,1)S(1)} %copy.45, s32[]{:T(128)} %constant.145.clone.1, s32[]{:T(128)} %constant.145.clone.1, s32[]{:T(128)} %constant.145.clone.1, s32[]{:T(128)S(6)} %select_n.117) | dynamic-update-slice | bytes 184516 | tf_op jit(solution)/shard_map/dynamic_update_slice | solution.py:48
  666.6 162.5 %dynamic_update_slice.68 = bf16[31,31,1,768]{3,2,1,0:T(2,128)(2,1)} dynamic-update-slice(bf16[31,31,1,768]{3,2,1,0:T(2,128)(2,1)} %dynamic_update_slice.67, bf16[31,31,1,48]{3,2,1,0:T(2,128)(2,1)S(1)} %copy.46, s32[]{:T(128)} %constant.145.clone.1, s32[]{:T(128)} %constant.145.clone.1, s32[]{:T(128)} %constant.145.clone.1, s32[]{:T(128)S(6)} %select_n.119) | dynamic-update-slice | bytes 184516 | tf_op jit(solution)/shard_map/dynamic_update_slice | solution.py:53
  830.5 1.3 copy.48
  831.8 162.8 %dynamic_update_slice.69 = bf16[31,31,1,768]{3,2,1,0:T(2,128)(2,1)} dynamic-update-slice(bf16[31,31,1,768]{3,2,1,0:T(2,128)(2,1)} %dynamic_update_slice.68, bf16[31,31,1,48]{3,2,1,0:T(2,128)(2,1)S(1)} %copy.47, s32[]{:T(128)} %constant.145.clone.1, s32[]{:T(128)} %constant.145.clone.1, s32[]{:T(128)} %constant.145.clone.1, s32[]{:T(128)S(6)} %select_n.121) | dynamic-update-slice | bytes 184516 | tf_op jit(solution)/shard_map/dynamic_update_slice | solution.py:48
  994.6 162.5 %dynamic_update_slice.70 = bf16[31,31,1,768]{3,2,1,0:T(2,128)(2,1)} dynamic-update-slice(bf16[31,31,1,768]{3,2,1,0:T(2,128)(2,1)} %dynamic_update_slice.69, bf16[31,31,1,48]{3,2,1,0:T(2,128)(2,1)S(1)} %copy.48, s32[]{:T(128)} %constant.145.clone.1, s32[]{:T(128)} %constant.145.clone.1, s32[]{:T(128)} %constant.145.clone.1, s32[]{:T(128)S(6)} %select_n.123) | dynamic-update-slice | bytes 184516 | tf_op jit(solution)/shard_map/dynamic_update_slice | solution.py:53
  1158.4 1.3 copy.50
  1159.7 162.5 %dynamic_update_slice.71 = bf16[31,31,1,768]{3,2,1,0:T(2,128)(2,1)} dynamic-update-slice(bf16[31,31,1,768]{3,2,1,0:T(2,128)(2,1)} %dynamic_update_slice.70, bf16[31,31,1,48]{3,2,1,0:T(2,128)(2,1)S(1)} %copy.49, s32[]{:T(128)} %constant.145.clone.1, s32[]{:T(128)} %constant.145.clone.1, s32[]{:T(128)} %constant.145.clone.1, s32[]{:T(128)S(6)} %select_n.125) | dynamic-update-slice | bytes 184516 | tf_op jit(solution)/shard_map/dynamic_update_slice | solution.py:48
  1322.3 162.5 %dynamic_update_slice.72 = bf16[31,31,1,768]{3,2,1,0:T(2,128)(2,1)} dynamic-update-slice(bf16[31,31,1,768]{3,2,1,0:T(2,128)(2,1)} %dynamic_update_slice.71, bf16[31,31,1,48]{3,2,1,0:T(2,128)(2,1)S(1)} %copy.50, s32[]{:T(128)} %constant.145.clone.1, s32[]{:T(128)} %constant.145.clone.1, s32[]{:T(128)} %constant.145.clone.1, s32[]{:T(128)S(6)} %select_n.127) | dynamic-update-slice | bytes 184516 | tf_op jit(solution)/shard_map/dynamic_update_slice | solution.py:53
  1486.1 1.3 copy.52
  1487.5 162.5 %dynamic_update_slice.73 = bf16[31,31,1,768]{3,2,1,0:T(2,128)(2,1)} dynamic-update-slice(bf16[31,31,1,768]{3,2,1,0:T(2,128)(2,1)} %dynamic_update_slice.72, bf16[31,31,1,48]{3,2,1,0:T(2,128)(2,1)S(1)} %copy.51, s32[]{:T(128)} %constant.145.clone.1, s32[]{:T(128)} %constant.145.clone.1, s32[]{:T(128)} %constant.145.clone.1, s32[]{:T(128)S(6)} %select_n.129) | dynamic-update-slice | bytes 184516 | tf_op jit(solution)/shard_map/dynamic_update_slice | solution.py:48
  1650.0 162.9 %dynamic_update_slice.74 = bf16[31,31,1,768]{3,2,1,0:T(2,128)(2,1)} dynamic-update-slice(bf16[31,31,1,768]{3,2,1,0:T(2,128)(2,1)} %dynamic_update_slice.73, bf16[31,31,1,48]{3,2,1,0:T(2,128)(2,1)S(1)} %copy.52, s32[]{:T(128)} %constant.145.clone.1, s32[]{:T(128)} %constant.145.clone.1, s32[]{:T(128)} %constant.145.clone.1, s32[]{:T(128)S(6)} %select_n.131) | dynamic-update-slice | bytes 184516 | tf_op jit(solution)/shard_map/dynamic_update_slice | solution.py:53
  1815.6 162.6 %dynamic_update_slice.75 = bf16[31,31,1,768]{3,2,1,0:T(2,128)(2,1)} dynamic-update-slice(bf16[31,31,1,768]{3,2,1,0:T(2,128)(2,1)} %dynamic_update_slice.74, bf16[31,31,1,48]{3,2,1,0:T(2,128)(2,1)S(1)} %copy.53, s32[]{:T(128)} %constant.145.clone.1, s32[]{:T(128)} %constant.145.clone.1, s32[]{:T(128)} %constant.145.clone.1, s32[]{:T(128)S(6)} %select_n.133) | dynamic-update-slice | bytes 184516 | tf_op jit(solution)/shard_map/dynamic_update_slice | solution.py:48
  1978.1 162.5 %dynamic_update_slice.76 = bf16[31,31,1,768]{3,2,1,0:T(2,128)(2,1)} dynamic-update-slice(bf16[31,31,1,768]{3,2,1,0:T(2,128)(2,1)} %dynamic_update_slice.75, bf16[31,31,1,48]{3,2,1,0:T(2,128)(2,1)S(1)} %copy.54, s32[]{:T(128)} %constant.145.clone.1, s32[]{:T(128)} %constant.145.clone.1, s32[]{:T(128)} %constant.145.clone.1, s32[]{:T(128)S(6)} %select_n.135) | dynamic-update-slice | bytes 184516 | tf_op jit(solution)/shard_map/dynamic_update_slice | solution.py:53
  2141.0 1.3 copy.56
  2142.4 162.6 %dynamic_update_slice.77 = bf16[31,31,1,768]{3,2,1,0:T(2,128)(2,1)} dynamic-update-slice(bf16[31,31,1,768]{3,2,1,0:T(2,128)(2,1)} %dynamic_update_slice.76, bf16[31,31,1,48]{3,2,1,0:T(2,128)(2,1)S(1)} %copy.55, s32[]{:T(128)} %constant.145.clone.1, s32[]{:T(128)} %constant.145.clone.1, s32[]{:T(128)} %constant.145.clone.1, s32[]{:T(128)S(6)} %select_n.137) | dynamic-update-slice | bytes 184516 | tf_op jit(solution)/shard_map/dynamic_update_slice | solution.py:48
  2304.9 162.5 %dynamic_update_slice.78 = bf16[31,31,1,768]{3,2,1,0:T(2,128)(2,1)} dynamic-update-slice(bf16[31,31,1,768]{3,2,1,0:T(2,128)(2,1)} %dynamic_update_slice.77, bf16[31,31,1,48]{3,2,1,0:T(2,128)(2,1)S(1)} %copy.56, s32[]{:T(128)} %constant.145.clone.1, s32[]{:T(128)} %constant.145.clone.1, s32[]{:T(128)} %constant.145.clone.1, s32[]{:T(128)S(6)} %select_n.139) | dynamic-update-slice | bytes 184516 | tf_op jit(solution)/shard_map/dynamic_update_slice | solution.py:53
  2468.8 34.8 %dynamic_update_slice.79 = bf16[31,31,1,768]{3,2,1,0:T(2,128)(2,1)} dynamic-update-slice(bf16[31,31,1,768]{3,2,1,0:T(2,128)(2,1)} %dynamic_update_slice.78, bf16[31,31,1,48]{3,2,1,0:T(2,128)(2,1)S(1)} %copy.57, s32[]{:T(128)} %constant.145.clone.1, s32[]{:T(128)} %constant.145.clone.1, s32[]{:T(128)} %constant.145.clone.1, s32[]{:T(128)S(6)} %select_n.141) | dynamic-update-slice | bytes 184516 | tf_op jit(solution)/shard_map/dynamic_update_slice | solution.py:48
  2503.6 1.6 copy.40
  2505.2 1.6 copy.41
  2506.8 1.4 maximum_bitcast_fusion
  2508.6 75.6 %fusion = f32[1,16,16,768]{3,0,2,1:T(1,128)S(1)} fusion(bf16[31,31,1,768]{3,2,1,0:T(2,128)(2,1)S(1)} %copy-done.2, bf16[1,46,46,768]{3,2,1,0:T(8,128)(2,1)S(1)} %maximum_bitcast_fusion), kind=kOutput, calls=%fused_computation | convolution fusion | flops 377880576 | bytes 5512704 | tf_op jit(solution)/shard_map/conv_general_dilated | solution.py:61
  2585.0 7.7 fusion.12
  (72 shorter events, 21.0 us)
Async XLA Ops:
  6.5 5.7 copy-start
  6.5 2578.5 %all-gather.3.cloned.1.call-start = ((), (), s32[]{:S(2)}) async-start(), calls=%async_computation | async-start | bytes 2506752 | tf_op jit(solution)/shard_map/all_gather | solution.py:75
  7.3 2577.8 %all-gather.5.cloned.1.call-start = ((), (), s32[]{:S(2)}) async-start(), calls=%async_computation.1 | async-start | bytes 2506752 | tf_op jit(solution)/shard_map/all_gather | solution.py:76
  8.5 3.7 collective-permute-start
  10.9 5.7 collective-permute-start.1
  17.4 7.3 copy-start.3
  17.4 2486.2 %collective-permute-start.2 = (bf16[46,15,768]{2,0,1:T(8,128)(2,1)S(1)}, bf16[46,15,768]{2,0,1:T(8,128)(2,1)}, u32[]{:S(2)}, u32[]{:S(2)}) collective-permute-start(bf16[46,15,768]{2,0,1:T(8,128)(2,1)S(1)} %copy.38), channel_id=1, source_target_pairs={{0,1},{1,2},{2,3},{4,5},{5,6},{6,7},{8,9},{9,10},{10,11},{12,13},{... | collective-permute-start | bytes 3179528 | tf_op jit(solution)/shard_map/ppermute | solution.py:12
  23.5 2481.7 %collective-permute-start.3 = (bf16[46,15,768]{2,0,1:T(8,128)(2,1)}, bf16[46,15,768]{2,0,1:T(8,128)(2,1)}, u32[]{:S(2)}, u32[]{:S(2)}) collective-permute-start(bf16[46,15,768]{2,0,1:T(8,128)(2,1)} %copy.39), channel_id=1, source_target_pairs={{1,0},{2,1},{3,2},{5,4},{6,5},{7,6},{9,8},{10,9},{11,10},{13,12},{... | collective-permute-start | bytes 3179528 | tf_op jit(solution)/shard_map/ppermute | solution.py:15
  24.8 42.2 %collective-permute-start.4 = (bf16[31,31,48]{2,1,0:T(8,128)(2,1)S(1)}, bf16[31,31,48]{2,1,0:T(8,128)(2,1)}, u32[]{:S(2)}, u32[]{:S(2)}) collective-permute-start(bf16[31,31,48]{2,1,0:T(8,128)(2,1)S(1)} %copy-done.3), channel_id=1, source_target_pairs={{0,1},{1,2},{2,3},{3,4},{4,5},{5,6},{6,7},{7,8},{8,9},{9,10},{10,1... | collective-permute-start | bytes 276776 | tf_op jit(solution)/shard_map/ppermute | solution.py:45
  27.5 41.8 %collective-permute-start.5 = (bf16[31,31,48]{2,1,0:T(8,128)(2,1)S(1)}, bf16[31,31,48]{2,1,0:T(8,128)(2,1)S(1)}, u32[]{:S(2)}, u32[]{:S(2)}) collective-permute-start(bf16[31,31,48]{2,1,0:T(8,128)(2,1)S(1)} %copy-done.3), channel_id=1, source_target_pairs={{0,15},{1,0},{2,1},{3,2},{4,3},{5,4},{6,5},{7,6},{8,7},{9,8},{10,9... | collective-permute-start | bytes 276776 | tf_op jit(solution)/shard_map/ppermute | solution.py:50
  66.9 11.4 collective-permute-start.6
  69.3 65.8 %copy-start.4 = (bf16[31,31,48]{2,1,0:T(8,128)(2,1)}, bf16[31,31,48]{2,1,0:T(8,128)(2,1)S(1)}, u32[]{:S(2)}) copy-start(bf16[31,31,48]{2,1,0:T(8,128)(2,1)S(1)} %collective-permute-done.5) | copy-start | bytes 276772
  69.3 11.6 collective-permute-start.7
  78.4 11.0 collective-permute-start.8
  80.8 54.3 %copy-start.6 = (bf16[31,31,48]{2,1,0:T(8,128)(2,1)}, bf16[31,31,48]{2,1,0:T(8,128)(2,1)S(1)}, u32[]{:S(2)}) copy-start(bf16[31,31,48]{2,1,0:T(8,128)(2,1)S(1)} %collective-permute-done.7) | copy-start | bytes 276772
  80.8 13.5 collective-permute-start.9
  89.4 10.9 collective-permute-start.10
  94.4 40.7 %copy-start.8 = (bf16[31,31,48]{2,1,0:T(8,128)(2,1)}, bf16[31,31,48]{2,1,0:T(8,128)(2,1)S(1)}, u32[]{:S(2)}) copy-start(bf16[31,31,48]{2,1,0:T(8,128)(2,1)S(1)} %collective-permute-done.9) | copy-start | bytes 276772
  94.4 13.1 collective-permute-start.11
  100.3 34.8 %copy-start.5 = (bf16[31,31,48]{2,1,0:T(8,128)(2,1)}, bf16[31,31,48]{2,1,0:T(8,128)(2,1)S(1)}, u32[]{:S(2)}) copy-start(bf16[31,31,48]{2,1,0:T(8,128)(2,1)S(1)} %collective-permute-done.10) | copy-start | bytes 276772
  100.3 11.2 collective-permute-start.12
  107.5 27.6 %copy-start.10 = (bf16[31,31,48]{2,1,0:T(8,128)(2,1)}, bf16[31,31,48]{2,1,0:T(8,128)(2,1)S(1)}, u32[]{:S(2)}) copy-start(bf16[31,31,48]{2,1,0:T(8,128)(2,1)S(1)} %collective-permute-done.11) | copy-start | bytes 276772
  107.5 13.8 collective-permute-start.13
  111.5 23.7 copy-start.7
  111.5 11.8 collective-permute-start.14
  121.3 13.8 copy-start.11
  121.3 12.5 collective-permute-start.15
  123.2 11.9 copy-start.9
  123.2 11.9 collective-permute-start.16
  133.8 2007.2 %collective-permute-start.17 = (bf16[31,31,48]{2,1,0:T(8,128)(2,1)}, bf16[31,31,48]{2,1,0:T(8,128)(2,1)}, u32[]{:S(2)}, u32[]{:S(2)}) collective-permute-start(bf16[31,31,48]{2,1,0:T(8,128)(2,1)} %collective-permute-done.15), channel_id=1, source_target_pairs={{0,15},{1,0},{2,1},{3,2},{4,3},{5,4},{6,5},{7,6},{8,7},{9,8},{10,9... | collective-permute-start | bytes 276776 | tf_op jit(solution)/shard_map/ppermute | solution.py:50
  135.2 2332.3 %collective-permute-start.18 = (bf16[31,31,48]{2,1,0:T(8,128)(2,1)S(1)}, bf16[31,31,48]{2,1,0:T(8,128)(2,1)}, u32[]{:S(2)}, u32[]{:S(2)}) collective-permute-start(bf16[31,31,48]{2,1,0:T(8,128)(2,1)S(1)} %collective-permute-done.16), channel_id=1, source_target_pairs={{0,1},{1,2},{2,3},{3,4},{4,5},{5,6},{6,7},{7,8},{8,9},{9,10},{10,1... | collective-permute-start | bytes 276776 | tf_op jit(solution)/shard_map/ppermute | solution.py:45
  2506.8 1.8 copy-start.2
  2508.6 75.6 %copy-start.1 = (bf16[16,16,768]{2,1,0:T(8,128)(2,1)S(1)}, bf16[16,16,768]{2,1,0:T(8,128)(2,1)}, u32[]{:S(2)}) copy-start(bf16[16,16,768]{2,1,0:T(8,128)(2,1)} %param.4) | copy-start | bytes 1179652
Sparse Core Ops, SparseCore 0:
  9.6 50.2 all-gather.2
  136.1 60.7 all-gather.4
